TPU v7x, 32 devices: a whole 2x2x4 slice. The times are simulated.
32 devices in a mesh: rows: 8 (over z, y), grp: 4 (over x, core).
Axes of the slice: x: 2, y: 2, z: 4, core: 2. Of those that a mesh axis runs over, the one named last changes fastest.
Arguments:
- panel: float32 [8192, 256], P(('rows', 'grp')), may hold values from -6000 to 6000
- trailing: float32 [8192, 2048], P(('rows', 'grp')), may hold values from -6000 to 6000
Outputs:
- upper_panel: float32 [256, 256], replicated
- projection: float32 [256, 2048], replicated
- updated: float32 [8192, 2048], P(('rows', 'grp'))
- upper_next: float32 [256, 256], replicated
All inputs are finite; a program needn't handle non-finite values.
Results may differ from a plain program's by a relative error of at most 0.00019.
Values sent between devices are 32-bit elements; how exact they have to be, the bound alone decides.
A program may use at most 128 MiB of HBM per device.

v0:
```python
import jax
import jax.numpy as jnp
from jax import lax
from jax.sharding import PartitionSpec as P


def cross(left, right):
    return lax.dot_general(
        left,
        right,
        (((0,), (0,)), ((), ())),
        precision=lax.Precision.HIGHEST,
        preferred_element_type=jnp.float32,
    )


def product(left, right):
    return jnp.dot(left, right, precision=lax.Precision.HIGHEST, preferred_element_type=jnp.float32)


def lower_inverse(lower):
    order = lower.shape[0]
    result = jnp.zeros((order, order), jnp.float32)
    for index in range(order):
        unit = (jnp.arange(order) == index).astype(jnp.float32)
        new_row = (
            unit - jnp.dot(lower[index, :], result, precision=lax.Precision.HIGHEST)
        ) / lower[index, index]
        result = result.at[index, :].set(new_row)
    return result


def factor_pair(matrix):
    order = matrix.shape[0]
    if order <= 16 or order % 2 == 1:
        lower = jnp.zeros((order, order), jnp.float32)
        row_ids = jnp.arange(order)
        for index in range(order):
            column = matrix[:, index] - jnp.dot(
                lower, lower[index, :], precision=lax.Precision.HIGHEST
            )
            pivot = jnp.sqrt(column[index])
            lower = lower.at[:, index].set(jnp.where(row_ids >= index, column / pivot, 0.0))
        return (lower, lower_inverse(lower))
    middle = order // 2
    first_low, first_inv = factor_pair(matrix[:middle, :middle])
    below = product(matrix[middle:, :middle], first_inv.T)
    schur = matrix[middle:, middle:] - product(below, below.T)
    second_low, second_inv = factor_pair(schur)
    below_inv = -product(second_inv, product(below, first_inv))
    zeros_block = jnp.zeros((middle, order - middle), jnp.float32)
    lower = jnp.concatenate(
        [
            jnp.concatenate([first_low, zeros_block], axis=1),
            jnp.concatenate([below, second_low], axis=1),
        ],
        axis=0,
    )
    inverse = jnp.concatenate(
        [
            jnp.concatenate([first_inv, zeros_block], axis=1),
            jnp.concatenate([below_inv, second_inv], axis=1),
        ],
        axis=0,
    )
    return (lower, inverse)


def upper_of(matrix):
    return factor_pair(matrix)[0].T


def per_device(panel, trailing):
    inv_rows = 1.0 / (panel.shape[0] * lax.axis_size(("rows", "grp")))
    width = panel.shape[1]
    gram_panel, cross_terms, gram_head = lax.psum(
        (
            cross(panel, panel),
            cross(panel, trailing),
            cross(trailing[:, :width], trailing[:, :width]),
        ),
        ("rows", "grp"),
    )
    lower, lower_inv = factor_pair(gram_panel * inv_rows)
    upper_panel = lower.T
    inverse = lower_inv.T
    ortho_basis = product(panel, inverse)
    projection = cross(inverse, cross_terms) * inv_rows
    updated = trailing - product(ortho_basis, projection)
    head_proj = projection[:, :width]
    upper_next = upper_of(gram_head * inv_rows - cross(head_proj, head_proj))
    return (upper_panel, projection, updated, upper_next)


def solution(mesh):
    return jax.shard_map(
        per_device,
        mesh=mesh,
        in_specs=(P(("rows", "grp"), None), P(("rows", "grp"), None)),
        out_specs=(P(), P(), P(("rows", "grp"), None), P()),
        check_vma=False,
    )
```

profile of v0, /device:TPU:0, one launch (start us, length us, event | category | flops | bytes accessed | tf_op | source)
XLA Modules:
  0.0 1853.8 jit_solution(8966382655848866502)
XLA Ops:
  7.2 2.4 fusion.1984
  9.6 4.8 fusion.2984
  25.9 130.2 %all-reduce.122.cloned.1.call-done = (f32[256,256]{1,0:T(8,128)}, f32[256,2048]{1,0:T(8,128)}, f32[256,256]{1,0:T(8,128)}) async-done(((f32[256,256]{1,0:T(8,128)}, f32[256,2048]{1,0:T(8,128)}, f32[256,256]{1,0:T(8,128)}), (f32[256,256]{1,0:T(8,128)}, f32[256,2048]{1,0:T(8,128)}, f32[256,256]{1,0:T(8,128)})) %all-reduce.122.cloned.1.call-update) | async-done | bytes 2621456 | tf_op jit(solution)/shard_map/psum | solution.py:76
  195.2 1.5 fusion.981
  196.7 1.5 fusion.983
  198.2 1.5 fusion.985
  204.1 1.5 fusion.993
  207.0 1.5 fusion.997
  210.0 1.5 fusion.1001
  211.5 1.5 fusion.1003
  213.0 1.5 fusion.1005
  305.8 1.5 fusion.1047
  307.3 1.5 fusion.1049
  308.7 1.5 fusion.1051
  314.6 1.5 fusion.1059
  317.5 1.5 fusion.1063
  319.1 1.5 fusion.1065
  320.6 1.5 fusion.1067
  322.1 1.5 fusion.1069
  571.1 1.5 fusion.1215
  577.0 1.5 fusion.1223
  578.5 1.5 fusion.1225
  580.0 1.5 fusion.1227
  581.5 1.5 fusion.1229
  774.8 1.5 fusion.1335
  783.5 1.5 fusion.1347
  788.0 1.5 fusion.1353
  789.5 1.5 fusion.1355
  791.0 1.5 fusion.1357
  983.4 1.5 fusion.1463
  986.3 1.5 fusion.1467
  992.2 1.5 fusion.1475
  993.7 1.5 fusion.1477
  995.1 1.5 fusion.1479
  996.7 1.5 fusion.1481
  998.2 1.5 fusion.1483
  999.7 1.5 fusion.1485
  1003.9 1.9 convolution_multiply_fusion
  1196.8 1.5 fusion.1591
  1205.6 1.5 fusion.1603
  1211.4 1.5 fusion.1611
  1212.9 1.5 fusion.1613
  1214.4 1.5 fusion.1615
  1406.4 1.5 fusion.1719
  1413.7 1.5 fusion.1729
  1415.2 1.5 fusion.1731
  1418.2 1.5 fusion.1735
  1421.1 1.5 fusion.1739
  1422.6 1.5 fusion.1741
  1424.1 1.5 fusion.1743
  1615.9 1.5 fusion.1847
  1621.8 1.5 fusion.1855
  1623.2 1.4 fusion.1857
  1624.7 1.5 fusion.1859
  1627.7 1.5 fusion.1863
  1630.6 1.5 fusion.1867
  1632.1 1.5 fusion.1869
  1633.6 1.5 fusion.1871
  1788.3 1.5 fusion.1951
  1789.8 1.5 fusion.1953
  1795.7 1.5 fusion.1961
  1797.1 1.5 fusion.1963
  1798.6 1.5 fusion.1965
  1840.4 4.9 convolution_subtract_fusion
  (4251 shorter events, 1266.1 us)
Async XLA Ops:
  7.2 2.5 copy-start
  7.2 148.9 %all-reduce.122.cloned.1.call-start = ((), (), s32[]{:S(2)}) async-start(), calls=%async_computation | async-start | bytes 5242880 | tf_op jit(solution)/shard_map/psum | solution.py:76
  157.6 1578.2 %copy-start.35 = (f32[16]{0:T(128)}, f32[16]{0:T(128)S(1)}, u32[]{:S(2)}) copy-start(f32[16]{0:T(128)S(1)} %get-tuple-element.13089) | copy-start | bytes 196
  192.9 2.3 copy-start.8
  302.1 2.2 copy-start.10
  325.1 52.1 %copy-start.24 = (f32[16,16]{1,0:T(8,128)}, f32[16,16]{1,0:T(8,128)S(1)}, u32[]{:S(2)}) copy-start(f32[16,16]{1,0:T(8,128)S(1)} %fusion.2173) | copy-start | bytes 3076
  561.5 2.3 copy-start.4
  734.8 59.3 %copy-start.26 = (f32[16,16]{1,0:T(8,128)}, f32[16,16]{1,0:T(8,128)S(1)}, u32[]{:S(2)}) copy-start(f32[16,16]{1,0:T(8,128)S(1)} %fusion.2165) | copy-start | bytes 3076
  771.1 2.2 copy-start.12
  893.9 110.0 %copy-start.20 = (f32[256,2048]{1,0:T(8,128)S(1)}, f32[256,2048]{1,0:T(8,128)}, u32[]{:S(2)}) copy-start(f32[256,2048]{1,0:T(8,128)} %get-tuple-element.12621) | copy-start | bytes 6291460
  943.6 62.3 %copy-start.22 = (f32[16,16]{1,0:T(8,128)}, f32[16,16]{1,0:T(8,128)S(1)}, u32[]{:S(2)}) copy-start(f32[16,16]{1,0:T(8,128)S(1)} %fusion.2161) | copy-start | bytes 3076
  979.7 2.2 copy-start.1
  1003.9 3.3 copy-start.21
  1005.8 1.3 copy-start.19
  1156.9 59.4 %copy-start.28 = (f32[16,16]{1,0:T(8,128)}, f32[16,16]{1,0:T(8,128)S(1)}, u32[]{:S(2)}) copy-start(f32[16,16]{1,0:T(8,128)S(1)} %fusion.2157) | copy-start | bytes 3076
  1193.1 2.3 copy-start.14
  1402.7 2.2 copy-start.6
  1575.8 59.4 %copy-start.29 = (f32[16,16]{1,0:T(8,128)}, f32[16,16]{1,0:T(8,128)S(1)}, u32[]{:S(2)}) copy-start(f32[16,16]{1,0:T(8,128)S(1)} %fusion.2149) | copy-start | bytes 3076
  1612.2 2.3 copy-start.16
  1695.9 79.1 %copy-start.9 = (f32[16,16]{1,0:T(8,128)S(1)}, f32[16,16]{1,0:T(8,128)}, u32[]{:S(2)}) copy-start(f32[16,16]{1,0:T(8,128)} %copy-done.8) | copy-start | bytes 3076
  1752.9 84.1 %copy-start.15 = (f32[16,16]{1,0:T(8,128)S(1)}, f32[16,16]{1,0:T(8,128)}, u32[]{:S(2)}) copy-start(f32[16,16]{1,0:T(8,128)} %copy-done.14) | copy-start | bytes 3076
  1756.7 81.2 %copy-start.17 = (f32[16,16]{1,0:T(8,128)S(1)}, f32[16,16]{1,0:T(8,128)}, u32[]{:S(2)}) copy-start(f32[16,16]{1,0:T(8,128)} %copy-done.16) | copy-start | bytes 3076
  1759.1 79.5 %copy-start.7 = (f32[16,16]{1,0:T(8,128)S(1)}, f32[16,16]{1,0:T(8,128)}, u32[]{:S(2)}) copy-start(f32[16,16]{1,0:T(8,128)} %copy-done.6) | copy-start | bytes 3076
  1772.5 29.9 %copy-start.36 = (f32[16]{0:T(128)S(1)}, f32[16]{0:T(128)}, u32[]{:S(2)}) copy-start(f32[16]{0:T(128)} %copy-done.35) | copy-start | bytes 196
  1773.8 64.8 %copy-start.30 = (f32[32,32]{1,0:T(8,128)S(1)}, f32[32,32]{1,0:T(8,128)}, u32[]{:S(2)}) copy-start(f32[32,32]{1,0:T(8,128)} %select_maximum_fusion.23) | copy-start | bytes 12292
  1774.6 65.8 %copy-start.18 = (f32[256,2048]{1,0:T(8,128)S(1)}, f32[256,2048]{1,0:T(8,128)}, u32[]{:S(2)}) copy-start(f32[256,2048]{1,0:T(8,128)} %param.2019) | copy-start | bytes 6291460
  1775.0 62.8 %copy-start.34 = (f32[32,32]{1,0:T(8,128)S(1)}, f32[32,32]{1,0:T(8,128)}, u32[]{:S(2)}) copy-start(f32[32,32]{1,0:T(8,128)} %select_maximum_fusion.21) | copy-start | bytes 12292
  1776.6 62.2 %copy-start.31 = (f32[32,32]{1,0:T(8,128)S(1)}, f32[32,32]{1,0:T(8,128)}, u32[]{:S(2)}) copy-start(f32[32,32]{1,0:T(8,128)} %select_maximum_fusion.19) | copy-start | bytes 12292
  1778.8 2.3 copy-start.3
  1840.3 4.9 copy-start.11
  1840.3 4.9 copy-start.25
  1840.4 4.9 copy-start.32
  1840.4 5.0 copy-start.13
  1840.4 5.0 copy-start.27
  1840.4 5.0 copy-start.33
  1840.4 5.1 copy-start.5
  1840.4 5.2 copy-start.2
  1840.4 5.2 copy-start.23
Sparse Core Ops, SparseCore 0:
  15.8 140.1 all-reduce.121
where the time goes:
time: 1880 us; the launch traced here: 1850 us
  matrix products  562 us (30%)
  local copies, waits for them, and re-layouts  450 us (24%)
  between operations  356 us (19%)
  other arithmetic  355 us (19%)
  waiting for transfers between devices  130 us (7%)
    dot_general x496, matrix products, lower_inverse(): jnp.dot(lower[index, :], result, precision=lax.Precision.HIGHEST)  465 us
    another operation x943, other arithmetic  345 us
    slice x480, local copies, waits for them, and re-layouts, factor_pair(): pivot = jnp.sqrt(column[index])  288 us
    psum x1, waiting for transfers between devices, per_device(): lax.psum((cross(panel, panel), cross(panel, trailing), cross(trailing[:,...  130 us
    dot_general x481, matrix products, factor_pair(): jnp.dot(lower, lower[index, :], precision=lax.Precision.HIGHEST)  63.9 us
    scatter x512, local copies, waits for them, and re-layouts, factor_pair(): lower.at[:, index].set(jnp.where(row_ids >= index, column / pivot, 0.0))  43.8 us
    another operation x512, local copies, waits for them, and re-layouts  43.5 us
    slice x62, local copies, waits for them, and re-layouts, lower_inverse(): lower[index, index]  41.8 us

commit v1 on v0

--- a/solution.py
+++ b/solution.py
@@ -74,12 +74,15 @@
     inv_rows = 1.0 / (panel.shape[0] * lax.axis_size(("rows", "grp")))
     width = panel.shape[1]
     gram_panel, cross_terms, gram_head = lax.psum(
-        (
-            cross(panel, panel),
-            cross(panel, trailing),
-            cross(trailing[:, :width], trailing[:, :width]),
+        lax.psum(
+            (
+                cross(panel, panel),
+                cross(panel, trailing),
+                cross(trailing[:, :width], trailing[:, :width]),
+            ),
+            "grp",
         ),
-        ("rows", "grp"),
+        "rows",
     )
     lower, lower_inv = factor_pair(gram_panel * inv_rows)
     upper_panel = lower.T

time: 1880 us -> 1930 us (1.027)
  waiting for transfers between devices: 130 us -> 173 us
    psum x0 -> x1, waiting for transfers between devices: none -> 110 us  [per_device(): lax.psum(lax.psum((cross(panel, panel), cross(panel, trailing), cross(tra...]
    psum x1, waiting for transfers between devices: 130 us -> 62.8 us  [per_device(): lax.psum((cross(panel, panel), cross(panel, trailing), cross(trailing[:,...]
where the time goes in v1:
time: 1930 us; the launch traced here: 1900 us
  matrix products  568 us (29%)
  local copies, waits for them, and re-layouts  453 us (23%)
  between operations  357 us (18%)
  other arithmetic  354 us (18%)
  waiting for transfers between devices  173 us (9%)
    dot_general x496, matrix products, lower_inverse(): jnp.dot(lower[index, :], result, precision=lax.Precision.HIGHEST)  471 us
    another operation x943, other arithmetic  345 us
    slice x480, local copies, waits for them, and re-layouts, factor_pair(): pivot = jnp.sqrt(column[index])  289 us
    psum x1, waiting for transfers between devices, per_device(): lax.psum(lax.psum((cross(panel, panel), cross(panel, trailing), cross(tra...  110 us
    dot_general x481, matrix products, factor_pair(): jnp.dot(lower, lower[index, :], precision=lax.Precision.HIGHEST)  63.9 us
    psum x1, waiting for transfers between devices, per_device(): lax.psum((cross(panel, panel), cross(panel, trailing), cross(trailing[:,...  62.8 us
    scatter x512, local copies, waits for them, and re-layouts, factor_pair(): lower.at[:, index].set(jnp.where(row_ids >= index, column / pivot, 0.0))  43.8 us
    slice x62, local copies, waits for them, and re-layouts, lower_inverse(): lower[index, index]  43.6 us

profile of v1, /device:TPU:0, one launch (start us, length us, event | category | flops | bytes accessed | tf_op | source)
XLA Modules:
  0.0 1904.9 jit_solution(5672085761019120734)
XLA Ops:
  7.2 2.4 fusion.1984
  9.6 4.8 fusion.2984
  15.8 62.8 %all-reduce.126.cloned.1.call-done = (f32[256,256]{1,0:T(8,128)}, f32[256,2048]{1,0:T(8,128)}, f32[256,256]{1,0:T(8,128)}) async-done(((f32[256,256]{1,0:T(8,128)}, f32[256,2048]{1,0:T(8,128)}, f32[256,256]{1,0:T(8,128)}), (f32[256,256]{1,0:T(8,128)}, f32[256,2048]{1,0:T(8,128)}, f32[256,256]{1,0:T(8,128)})) %all-reduce.126.cloned.1.call-update) | async-done | bytes 2621456 | tf_op jit(solution)/shard_map/psum | solution.py:77
  88.7 110.1 %all-reduce.124.cloned.1.call-done = (f32[256,256]{1,0:T(8,128)}, f32[256,2048]{1,0:T(8,128)}, f32[256,256]{1,0:T(8,128)}) async-done(((f32[256,256]{1,0:T(8,128)}, f32[256,2048]{1,0:T(8,128)}, f32[256,256]{1,0:T(8,128)}), (f32[256,256]{1,0:T(8,128)}, f32[256,2048]{1,0:T(8,128)}, f32[256,256]{1,0:T(8,128)})) %all-reduce.124.cloned.1.call-update) | async-done | bytes 2621456 | tf_op jit(solution)/shard_map/psum | solution.py:76
  241.0 1.5 fusion.985
  244.0 1.5 fusion.989
  245.5 1.5 fusion.991
  252.9 1.5 fusion.1001
  254.4 1.5 fusion.1003
  255.9 1.5 fusion.1005
  257.4 1.5 fusion.1007
  350.8 1.5 fusion.1049
  353.7 1.5 fusion.1053
  355.3 1.5 fusion.1055
  362.7 1.5 fusion.1065
  364.2 1.5 fusion.1067
  365.7 1.5 fusion.1069
  367.2 1.5 fusion.1071
  611.1 1.5 fusion.1209
  614.0 1.5 fusion.1213
  615.5 1.5 fusion.1215
  622.9 1.5 fusion.1225
  624.4 1.5 fusion.1227
  627.4 1.5 fusion.1231
  821.9 1.5 fusion.1337
  824.9 1.5 fusion.1341
  826.4 1.5 fusion.1343
  833.8 1.5 fusion.1353
  835.3 1.5 fusion.1355
  836.8 1.5 fusion.1357
  838.3 1.5 fusion.1359
  1032.0 1.5 fusion.1465
  1034.9 1.5 fusion.1469
  1036.5 1.5 fusion.1471
  1043.9 1.5 fusion.1481
  1045.4 1.5 fusion.1483
  1046.9 1.5 fusion.1485
  1048.3 1.5 fusion.1487
  1051.1 1.9 convolution_multiply_fusion
  1243.2 1.5 fusion.1589
  1246.1 1.5 fusion.1593
  1247.6 1.5 fusion.1595
  1255.0 1.5 fusion.1605
  1262.4 1.5 fusion.1615
  1453.4 1.5 fusion.1717
  1456.3 1.5 fusion.1721
  1457.8 1.5 fusion.1723
  1465.3 1.5 fusion.1733
  1469.7 1.5 fusion.1739
  1471.2 1.5 fusion.1741
  1472.7 1.5 fusion.1743
  1663.6 1.5 fusion.1845
  1666.5 1.5 fusion.1849
  1668.1 1.5 fusion.1851
  1675.5 1.5 fusion.1861
  1679.9 1.5 fusion.1867
  1681.4 1.5 fusion.1869
  1682.9 1.5 fusion.1871
  1830.4 1.5 fusion.1941
  1837.8 1.5 fusion.1951
  1840.7 1.5 fusion.1955
  1842.2 1.5 fusion.1957
  1849.6 1.5 fusion.1967
  1891.6 4.9 convolution_subtract_fusion
  (4254 shorter events, 1274.5 us)
Async XLA Ops:
  7.2 2.5 copy-start
  7.2 71.4 %all-reduce.126.cloned.1.call-start = ((), (), s32[]{:S(2)}) async-start(), calls=%async_computation.1 | async-start | bytes 5242880 | tf_op jit(solution)/shard_map/psum | solution.py:77
  15.7 183.1 %all-reduce.124.cloned.1.call-start = ((), (), s32[]{:S(2)}) async-start(), calls=%async_computation | async-start | bytes 5242880 | tf_op jit(solution)/shard_map/psum | solution.py:76
  200.4 1585.1 %copy-start.35 = (f32[16]{0:T(128)}, f32[16]{0:T(128)S(1)}, u32[]{:S(2)}) copy-start(f32[16]{0:T(128)S(1)} %get-tuple-element.13092) | copy-start | bytes 196
  235.8 2.3 copy-start.8
  345.6 2.3 copy-start.10
  368.8 52.3 %copy-start.24 = (f32[16,16]{1,0:T(8,128)}, f32[16,16]{1,0:T(8,128)S(1)}, u32[]{:S(2)}) copy-start(f32[16,16]{1,0:T(8,128)S(1)} %fusion.2173) | copy-start | bytes 3076
  605.8 2.3 copy-start.4
  780.4 59.8 %copy-start.26 = (f32[16,16]{1,0:T(8,128)}, f32[16,16]{1,0:T(8,128)S(1)}, u32[]{:S(2)}) copy-start(f32[16,16]{1,0:T(8,128)S(1)} %fusion.2165) | copy-start | bytes 3076
  816.7 2.3 copy-start.12
  940.5 110.6 %copy-start.20 = (f32[256,2048]{1,0:T(8,128)S(1)}, f32[256,2048]{1,0:T(8,128)}, u32[]{:S(2)}) copy-start(f32[256,2048]{1,0:T(8,128)} %get-tuple-element.12621) | copy-start | bytes 6291460
  990.6 62.5 %copy-start.22 = (f32[16,16]{1,0:T(8,128)}, f32[16,16]{1,0:T(8,128)S(1)}, u32[]{:S(2)}) copy-start(f32[16,16]{1,0:T(8,128)S(1)} %fusion.2161) | copy-start | bytes 3076
  1026.7 2.3 copy-start.1
  1051.1 3.3 copy-start.21
  1053.1 1.3 copy-start.19
  1204.8 59.5 %copy-start.28 = (f32[16,16]{1,0:T(8,128)}, f32[16,16]{1,0:T(8,128)S(1)}, u32[]{:S(2)}) copy-start(f32[16,16]{1,0:T(8,128)S(1)} %fusion.2157) | copy-start | bytes 3076
  1240.9 2.3 copy-start.14
  1451.1 2.3 copy-start.6
  1625.0 59.6 %copy-start.29 = (f32[16,16]{1,0:T(8,128)}, f32[16,16]{1,0:T(8,128)S(1)}, u32[]{:S(2)}) copy-start(f32[16,16]{1,0:T(8,128)S(1)} %fusion.2149) | copy-start | bytes 3076
  1661.3 2.3 copy-start.16
  1745.5 79.1 %copy-start.9 = (f32[16,16]{1,0:T(8,128)S(1)}, f32[16,16]{1,0:T(8,128)}, u32[]{:S(2)}) copy-start(f32[16,16]{1,0:T(8,128)} %copy-done.8) | copy-start | bytes 3076
  1802.7 85.5 %copy-start.15 = (f32[16,16]{1,0:T(8,128)S(1)}, f32[16,16]{1,0:T(8,128)}, u32[]{:S(2)}) copy-start(f32[16,16]{1,0:T(8,128)} %copy-done.14) | copy-start | bytes 3076
  1806.4 82.6 %copy-start.17 = (f32[16,16]{1,0:T(8,128)S(1)}, f32[16,16]{1,0:T(8,128)}, u32[]{:S(2)}) copy-start(f32[16,16]{1,0:T(8,128)} %copy-done.16) | copy-start | bytes 3076
  1808.8 81.0 %copy-start.7 = (f32[16,16]{1,0:T(8,128)S(1)}, f32[16,16]{1,0:T(8,128)}, u32[]{:S(2)}) copy-start(f32[16,16]{1,0:T(8,128)} %copy-done.6) | copy-start | bytes 3076
  1822.0 29.9 %copy-start.36 = (f32[16]{0:T(128)S(1)}, f32[16]{0:T(128)}, u32[]{:S(2)}) copy-start(f32[16]{0:T(128)} %copy-done.35) | copy-start | bytes 196
  1823.4 66.4 %copy-start.30 = (f32[32,32]{1,0:T(8,128)S(1)}, f32[32,32]{1,0:T(8,128)}, u32[]{:S(2)}) copy-start(f32[32,32]{1,0:T(8,128)} %select_maximum_fusion.23) | copy-start | bytes 12292
  1824.1 67.4 %copy-start.18 = (f32[256,2048]{1,0:T(8,128)S(1)}, f32[256,2048]{1,0:T(8,128)}, u32[]{:S(2)}) copy-start(f32[256,2048]{1,0:T(8,128)} %param.2019) | copy-start | bytes 6291460
  1824.6 64.4 %copy-start.34 = (f32[32,32]{1,0:T(8,128)S(1)}, f32[32,32]{1,0:T(8,128)}, u32[]{:S(2)}) copy-start(f32[32,32]{1,0:T(8,128)} %select_maximum_fusion.21) | copy-start | bytes 12292
  1826.1 63.8 %copy-start.31 = (f32[32,32]{1,0:T(8,128)S(1)}, f32[32,32]{1,0:T(8,128)}, u32[]{:S(2)}) copy-start(f32[32,32]{1,0:T(8,128)} %select_maximum_fusion.19) | copy-start | bytes 12292
  1828.3 2.1 copy-start.3
  1891.5 4.9 copy-start.11
  1891.5 4.9 copy-start.25
  1891.5 4.9 copy-start.32
  1891.5 5.0 copy-start.13
  1891.5 5.0 copy-start.27
  1891.5 5.0 copy-start.33
  1891.5 5.1 copy-start.5
  1891.6 5.2 copy-start.2
  1891.6 5.2 copy-start.23
Sparse Core Ops, SparseCore 0:
  15.9 62.6 all-reduce.125
  82.5 116.2 all-reduce.123
